TPU v7x, 32 devices: a whole 2x2x4 slice. The times are simulated.
32 devices in a mesh: leaf: 8 (over z, y), rows: 4 (over x, core).
Axes of the slice: x: 2, y: 2, z: 4, core: 2. Of those that a mesh axis runs over, the one named last changes fastest.
Arguments:
- sigma_top: float32 [2048, 1024], P('leaf'), may hold values from -4 to 40, as said below
- panel_top: float32 [1024, 12288], P(None, 'leaf'), may hold values from -0.125 to 0.125
- diag_top: float32 [12288, 256], P('leaf'), may hold values from -4 to 20, as said below
- panel_mid: float32 [1024, 24576], P(None, ('leaf', 'rows')), may hold values from -0.125 to 0.125
- diag_mid: float32 [24576, 256], P(('leaf', 'rows')), may hold values from -4 to 20, as said below
- pattern_mid: int32 [4, 4], replicated, may hold values from 0 to 23, as said below
- panel_low: float32 [1024, 49152], P(None, ('leaf', 'rows')), may hold values from -0.125 to 0.125
- diag_low: float32 [49152, 256], P(('leaf', 'rows')), may hold values from -4 to 20, as said below
- pattern_low: int32 [8, 4], replicated, may hold values from 0 to 23, as said below
Outputs:
- cross_top: float32 [1024, 12288], P('rows', 'leaf')
- marginal_top: float32 [12288, 256], P(('leaf', 'rows'))
- cross_mid: float32 [1024, 24576], P(None, ('leaf', 'rows'))
- marginal_mid: float32 [24576, 256], P(('leaf', 'rows'))
- cross_low: float32 [1024, 49152], P(None, ('leaf', 'rows'))
- marginal_low: float32 [49152, 256], P(('leaf', 'rows'))
Inputs may be any that keep to these rules, and one draw needn't show every extreme that they name: Each block of 1024 rows of sigma_top is symmetric. `diag_top`: each 256 x 256 block is symmetric. `diag_mid`: each block of 256 rows is symmetric. `diag_low`: each block of 256 rows is symmetric. `pattern_mid`: the 4 entries of a row are different; rows 2i and 2i + 1 together name 8 different blocks. `pattern_low`: the 4 entries of a row are different; rows 2i and 2i + 1 together name 8 different blocks.
All inputs are finite; a program needn't handle non-finite values.
Results may differ from a plain program's by a relative error of at most 0.00009.
Values sent between devices are 32-bit elements; how exact they have to be, the bound alone decides.
A program may use at most 192 MiB of HBM per device.

v0:
```python
import jax
import jax.numpy as jnp
from jax import lax
from jax.sharding import PartitionSpec as P

HIGH = lax.Precision.HIGHEST


def from_partner(value, axis, bit):
    return lax.ppermute(value, axis, [(i, i ^ 1 << bit) for i in range(lax.axis_size(axis))])


def block_diagonal(blocks):
    block_count = blocks.shape[0]
    block_side = blocks.shape[1]
    eye_table = jnp.eye(block_count, dtype=blocks.dtype)
    spread_out = blocks[:, :, None, :] * eye_table[:, None, :, None]
    return spread_out.reshape(block_count * block_side, block_count * block_side)


def select_blocks(panel_cols, diag_blocks, wanted, owned_mask, block_size):
    rows_total = panel_cols.shape[0]
    local_count = panel_cols.shape[1] // block_size
    taken_blocks = (
        jnp.take(panel_cols.reshape(rows_total, local_count, block_size), wanted, axis=1)
        * owned_mask[None, :, None]
    )
    taken_diag = (
        jnp.take(diag_blocks.reshape(local_count, block_size, block_size), wanted, axis=0)
        * owned_mask[:, None, None]
    )
    return (taken_blocks.reshape(rows_total, -1), taken_diag.reshape(-1, block_size))


def child_cov(parent_cov, chosen, chosen_diag, block_size):
    block_count = chosen_diag.shape[0] // block_size
    product = jnp.dot(parent_cov, chosen, precision=HIGH, preferred_element_type=jnp.float32)
    inner_part = jnp.dot(chosen.T, product, precision=HIGH, preferred_element_type=jnp.float32)
    return inner_part + block_diagonal(chosen_diag.reshape(block_count, block_size, block_size))


def marg_terms(panel_cols, cover_cols, block_size):
    rows_total = panel_cols.shape[0]
    block_count = panel_cols.shape[1] // block_size
    terms = jnp.einsum(
        "sai,saj->aij",
        panel_cols.reshape(rows_total, block_count, block_size),
        cover_cols.reshape(rows_total, block_count, block_size),
        precision=HIGH,
    )
    return terms.reshape(block_count * block_size, block_size)


def quad_total(pieces):
    for bit_number in range(2):
        others = from_partner((pieces[0], pieces[1], pieces[2]), "leaf", bit_number)
        pieces = (pieces[0] + others[0], pieces[1] + others[1], pieces[2] + others[2])
    return pieces


def local(
    sigma_top,
    panel_top,
    diag_top,
    panel_mid,
    diag_mid,
    pattern_mid,
    panel_low,
    diag_low,
    pattern_low,
):
    block_size = diag_top.shape[1]
    struct_rows = panel_top.shape[0]
    row_count = lax.axis_size("rows")
    leaf_index = lax.axis_index("leaf")
    rows_index = lax.axis_index("rows")
    slot_blocks = pattern_mid.shape[1]
    slot_width = slot_blocks * block_size
    quad_place = leaf_index % 4
    quad_number = leaf_index // 4
    top_local = panel_top.shape[1] // block_size
    children = 2 * quad_number + jnp.arange(2, dtype=jnp.int32)
    wanted_top = pattern_mid[children].reshape(-1)
    owned_top = (wanted_top // top_local == quad_place).astype(jnp.float32)
    chosen_top, chosen_top_diag = select_blocks(
        panel_top, diag_top, wanted_top % top_local, owned_top, block_size
    )
    padded_cov = lax.dynamic_update_slice_in_dim(
        jnp.zeros((struct_rows, struct_rows), jnp.float32),
        sigma_top,
        quad_place * sigma_top.shape[0],
        0,
    )
    share_rows = struct_rows // row_count
    diag_share = chosen_top_diag.shape[0] // row_count
    pieces = (
        lax.dynamic_slice_in_dim(padded_cov, rows_index * share_rows, share_rows, 0),
        lax.dynamic_slice_in_dim(chosen_top, rows_index * share_rows, share_rows, 0),
        lax.dynamic_slice_in_dim(chosen_top_diag, rows_index * diag_share, diag_share, 0),
    )
    pieces = quad_total(pieces)
    parent_cov, chosen_all, chosen_diag_all = (
        lax.all_gather(pieces[0], "rows", axis=0, tiled=True),
        lax.all_gather(pieces[1], "rows", axis=0, tiled=True),
        lax.all_gather(pieces[2], "rows", axis=0, tiled=True),
    )
    mid_local = panel_mid.shape[1] // block_size
    pair_number = leaf_index // 2
    pair_place = leaf_index % 2 * row_count + rows_index
    low_children = 2 * pair_number + jnp.arange(2, dtype=jnp.int32)
    wanted_mid = pattern_low[low_children].reshape(-1)
    owned_mid = (wanted_mid // mid_local == pair_place).astype(jnp.float32)
    chosen_mid, chosen_mid_diag = select_blocks(
        panel_mid, diag_mid, wanted_mid % mid_local, owned_mid, block_size
    )
    summed = lax.psum((chosen_mid, chosen_mid_diag), "rows")
    partner = from_partner((summed[0], summed[1]), "leaf", 0)
    mid_all = summed[0] + partner[0]
    mid_diag_all = summed[1] + partner[1]
    share_struct = struct_rows // row_count
    cov_rows = lax.dynamic_slice_in_dim(parent_cov, rows_index * share_struct, share_struct, 0)
    cross_top = -jnp.dot(cov_rows, panel_top, precision=HIGH, preferred_element_type=jnp.float32)
    panel_rows = lax.dynamic_slice_in_dim(panel_top, rows_index * share_struct, share_struct, 0)
    partial_value = marg_terms(panel_rows, cross_top, block_size)
    piece_rows = partial_value.shape[0] // row_count
    own_diag = lax.dynamic_slice_in_dim(diag_top, rows_index * piece_rows, piece_rows, 0)
    summed_terms = lax.psum(partial_value, "rows")
    marginal_top = own_diag - lax.dynamic_slice_in_dim(
        summed_terms, rows_index * piece_rows, piece_rows, 0
    )
    child_place = leaf_index // 2 % 2
    own_slots = lax.dynamic_slice_in_dim(chosen_all, child_place * slot_width, slot_width, 1)
    own_slot_diag = lax.dynamic_slice_in_dim(
        chosen_diag_all, child_place * slot_width, slot_width, 0
    )
    mid_cov = child_cov(parent_cov, own_slots, own_slot_diag, block_size)
    cross_mid = -jnp.dot(mid_cov, panel_mid, precision=HIGH, preferred_element_type=jnp.float32)
    marginal_mid = diag_mid - marg_terms(panel_mid, cross_mid, block_size)
    low_place = leaf_index % 2
    low_slots = lax.dynamic_slice_in_dim(mid_all, low_place * slot_width, slot_width, 1)
    low_slot_diag = lax.dynamic_slice_in_dim(mid_diag_all, low_place * slot_width, slot_width, 0)
    low_cov = child_cov(mid_cov, low_slots, low_slot_diag, block_size)
    cross_low = -jnp.dot(low_cov, panel_low, precision=HIGH, preferred_element_type=jnp.float32)
    marginal_low = diag_low - marg_terms(panel_low, cross_low, block_size)
    return (cross_top, marginal_top, cross_mid, marginal_mid, cross_low, marginal_low)


def solution(mesh):
    return jax.shard_map(
        local,
        mesh=mesh,
        in_specs=(
            P("leaf", None),
            P(None, "leaf"),
            P("leaf", None),
            P(None, ("leaf", "rows")),
            P(("leaf", "rows"), None),
            P(),
            P(None, ("leaf", "rows")),
            P(("leaf", "rows"), None),
            P(),
        ),
        out_specs=(
            P("rows", "leaf"),
            P(("leaf", "rows"), None),
            P(None, ("leaf", "rows")),
            P(("leaf", "rows"), None),
            P(None, ("leaf", "rows")),
            P(("leaf", "rows"), None),
        ),
        check_vma=False,
    )
```

profile of v0, /device:TPU:0, one launch (start us, length us, event | category | flops | bytes accessed | tf_op | source)
XLA Modules:
  0.0 711.9 jit_solution(2259707078649836408)
XLA Ops:
  11.7 23.2 %collective-permute-done = f32[256,1024]{1,0:T(8,128)S(1)} collective-permute-done((f32[256,1024]{1,0:T(8,128)S(1)}, f32[256,1024]{1,0:T(8,128)S(1)}, u32[]{:S(2)}, u32[]{:S(2)}) %collective-permute-start) | collective-permute-done | bytes 1048608 | tf_op jit(solution)/shard_map/ppermute | solution.py:10
  36.9 22.5 %collective-permute-done.1 = f32[256,1024]{1,0:T(8,128)S(1)} collective-permute-done((f32[256,1024]{1,0:T(8,128)S(1)}, f32[256,1024]{1,0:T(8,128)S(1)}, u32[]{:S(2)}, u32[]{:S(2)}) %collective-permute-start.1) | collective-permute-done | bytes 1048608 | tf_op jit(solution)/shard_map/ppermute | solution.py:10
  71.3 9.2 %copy.46 = f32[1024,8,256]{0,2,1:T(8,128)} copy(f32[1024,8,256]{2,0,1:T(8,128)} %bitcast.66) | data formatting | bytes 16777216 | tf_op jit(solution)/shard_map/jit(_take)/gather | solution.py:25
  86.5 5.9 fusion
  96.4 7.9 %convolution_negate_fusion.1 = f32[256,1536]{1,0:T(8,128)S(1)} fusion(f32[1024,1536]{1,0:T(8,128)} %param.10, f32[1024,1024]{1,0:T(8,128)} %all-gather.4.cloned.1.call-done, s32[]{:T(128)S(6)} %select_n.181), kind=kOutput, calls=%fused_computation.15 | convolution fusion | flops 4832231424 | bytes 8912900 | tf_op jit(solution)/shard_map/dot_general | solution.py:122
  110.5 6.6 copy.39
  117.8 6.6 copy.40
  124.4 7.1 %gather_fusion.1 = f32[8,1024,256]{2,1,0:T(8,128)} fusion(f32[1024,6,256]{2,0,1:T(8,128)} %copy.40, s32[1024]{0:T(1024)S(1)} %pad_clamp_fusion.2), kind=kCustom, calls=%fused_computation.1 | custom fusion | bytes 16777248 | tf_op jit(solution)/shard_map/jit(_take)/gather | solution.py:25
  131.5 9.2 %copy.41 = f32[1024,8,256]{0,2,1:T(8,128)} copy(f32[1024,8,256]{2,0,1:T(8,128)} %bitcast.67) | data formatting | bytes 16777216 | tf_op jit(solution)/shard_map/jit(_take)/gather | solution.py:25
  148.6 54.6 %collective-permute-done.4 = f32[512,256]{1,0:T(8,128)S(1)} collective-permute-done((f32[512,256]{1,0:T(8,128)S(1)}, f32[512,256]{1,0:T(8,128)S(1)}, u32[]{:S(2)}, u32[]{:S(2)}) %collective-permute-start.4) | collective-permute-done | bytes 524320 | tf_op jit(solution)/shard_map/ppermute | solution.py:10
  205.1 11.6 %collective-permute-done.5 = f32[512,256]{1,0:T(8,128)S(1)} collective-permute-done((f32[512,256]{1,0:T(8,128)S(1)}, f32[512,256]{1,0:T(8,128)S(1)}, u32[]{:S(2)}, u32[]{:S(2)}) %collective-permute-start.5) | collective-permute-done | bytes 524320 | tf_op jit(solution)/shard_map/ppermute | solution.py:10
  221.9 44.5 %collective-permute-done.3 = f32[256,2048]{0,1:T(8,128)S(1)} collective-permute-done((f32[256,2048]{0,1:T(8,128)S(1)}, f32[256,2048]{0,1:T(8,128)S(1)}, u32[]{:S(2)}, u32[]{:S(2)}) %collective-permute-start.3) | collective-permute-done | bytes 2097184 | tf_op jit(solution)/shard_map/ppermute | solution.py:10
  268.1 54.4 %all-reduce.3.cloned.1.call-done = (f32[1536,256]{1,0:T(8,128)}, f32[1024,2048]{0,1:T(8,128)}, f32[2048,256]{1,0:T(8,128)}) async-done(((f32[1536,256]{1,0:T(8,128)}, f32[1024,2048]{0,1:T(8,128)}, f32[2048,256]{1,0:T(8,128)}), (f32[1536,256]{1,0:T(8,128)}, f32[1024,2048]{0,1:T(8,128)}, f32[2048,256]{1,0:T(8,128)})) %all-reduce.3.cloned.1.call-update) | async-done | bytes 12058640 | tf_op jit(solution)/shard_map/psum | solution.py:127
  324.5 6.7 copy.48
  331.2 16.3 %all-gather.8.cloned.1.call-done = f32[2048,256]{1,0:T(8,128)} async-done(((f32[512,256]{1,0:T(8,128)}), f32[2048,256]{1,0:T(8,128)}) %all-gather.8.cloned.1.call-update) | async-done | bytes 2097168 | tf_op jit(solution)/shard_map/all_gather | solution.py:105
  350.7 198.7 %collective-permute-done.7 = f32[2048,256]{1,0:T(8,128)} collective-permute-done((f32[2048,256]{1,0:T(8,128)}, f32[2048,256]{1,0:T(8,128)}, u32[]{:S(2)}, u32[]{:S(2)}) %collective-permute-start.7) | collective-permute-done | bytes 2097184 | tf_op jit(solution)/shard_map/ppermute | solution.py:10
  558.5 25.9 %fusion.4 = f32[1024,1024]{1,0:T(8,128)S(1)} fusion(f32[1024,1024]{1,0:T(8,128)} %all-gather.4.cloned.1.call-done, f32[1024,2048]{0,1:T(8,128)} %all-gather.6.cloned.1.call-done, s32[]{:T(128)S(6)} %select_n.193), kind=kOutput, calls=%fused_computation.13 | convolution fusion | flops 12884901888 | bytes 12582916 | tf_op jit(solution)/shard_map/dot_general | solution.py:37
  584.4 14.0 %fusion.8 = f32[1024,1024]{1,0:T(8,128)S(1)} fusion(f32[1024,1024]{1,0:T(8,128)S(1)} %bitcast.75, f32[1024,1024]{1,0:T(8,128)S(1)} %fusion.4, f32[1024,2048]{0,1:T(8,128)S(1)} %copy-done.13, s32[]{:T(128)S(6)} %select_n.193), kind=kOutput, calls=%fused_computation.22 | convolution fusion | flops 12885950464 | bytes 16777220 | tf_op jit(solution)/shard_map/dot_general | solution.py:38
  600.4 12.4 %convolution_negate_fusion.2 = f32[1024,768]{0,1:T(8,128)} fusion(f32[1024,1024]{1,0:T(8,128)S(1)} %fusion.8, f32[1024,768]{1,0:T(8,128)S(1)} %copy-done.12), kind=kOutput, calls=%fused_computation.23 | convolution fusion | flops 9664462848 | bytes 10485760 | tf_op jit(solution)/shard_map/dot_general | solution.py:137
  623.3 17.4 %fusion.11 = f32[1024,1024]{1,0:T(8,128)S(1)} fusion(f32[1024,1024]{1,0:T(8,128)S(1)} %copy-done.4, f32[1024,2048]{0,1:T(8,128)} %collective-permute-done.6, s32[]{:T(128)S(6)} %select_n.204, f32[1024,2048]{0,1:T(8,128)} %get-tuple-element.25), kind=kOutput, calls=%fused_computation.25 | convolution fusion | flops 12885950464 | bytes 16777220 | tf_op jit(solution)/shard_map/dot_general | solution.py:37
  640.8 16.3 %fusion.12 = f32[1024,1024]{1,0:T(8,128)S(1)} fusion(f32[1024,1024]{1,0:T(8,128)S(1)} %fusion.11, f32[1024,2048]{0,1:T(8,128)} %collective-permute-done.6, s32[]{:T(128)S(6)} %select_n.204, f32[1024,2048]{0,1:T(8,128)S(1)} %bitcast.81), kind=kOutput, calls=%fused_computation.26 | convolution fusion | flops 12885950464 | bytes 16777220 | tf_op jit(solution)/shard_map/dot_general | solution.py:38
  657.1 22.3 %convolution_negate_fusion = f32[1024,1536]{1,0:T(8,128)} fusion(f32[1024,1536]{1,0:T(8,128)S(1)} %bitcast.83, f32[1024,1024]{1,0:T(8,128)S(1)} %fusion.12, f32[1024,1024]{1,0:T(8,128)S(1)} %bitcast.89), kind=kOutput, calls=%fused_computation.8 | convolution fusion | flops 19329974272 | bytes 20971520 | tf_op jit(solution)/shard_map/dot_general | solution.py:143
  679.4 6.6 copy.47
  686.0 17.6 %fusion.27 = f32[6,256,256]{1,2,0:T(8,128)S(1)} fusion(f32[1024,6,256]{0,2,1:T(8,128)} %bitcast.72, f32[1024,6,256]{0,2,1:T(8,128)} %bitcast.70), kind=kOutput, calls=%fused_computation.78 | convolution fusion | flops 4831838208 | bytes 14155776 | tf_op jit(solution)/shard_map/sai,saj->aij/dot_general | solution.py:45
  (132 shorter events, 79.7 us)
Async XLA Ops:
  7.2 109.9 %copy-start = (s32[4,4]{1,0:T(4,128)S(1)}, s32[4,4]{1,0:T(4,128)}, u32[]{:S(2)}) copy-start(s32[4,4]{1,0:T(4,128)} %param.14) | copy-start | bytes 196
  7.2 89.2 %all-gather.4.cloned.1.call-start = ((), (), s32[]{:S(2)}) async-start(), calls=%async_computation | async-start | bytes 5242880 | tf_op jit(solution)/shard_map/all_gather | solution.py:103
  8.6 52.0 %copy-start.17 = (s32[8,4]{0,1:T(4,128)S(1)}, s32[8,4]{0,1:T(4,128)}, u32[]{:S(2)}) copy-start(s32[8,4]{0,1:T(4,128)} %param.17) | copy-start | bytes 388
  8.6 52.9 %copy-start.11 = (f32[1024,768]{1,0:T(8,128)S(1)}, f32[1024,768]{1,0:T(8,128)}, u32[]{:S(2)}) copy-start(f32[1024,768]{1,0:T(8,128)} %param.12) | copy-start | bytes 9437188
  8.6 26.2 %collective-permute-start = (f32[256,1024]{1,0:T(8,128)S(1)}, f32[256,1024]{1,0:T(8,128)S(1)}, u32[]{:S(2)}, u32[]{:S(2)}) collective-permute-start(f32[256,1024]{1,0:T(8,128)S(1)} %constant_dynamic-slice_fusion.2), channel_id=1, source_target_pairs={{0,4},{4,0},{8,12},{12,8},{16,20},{20,16},{24,28},{28,24},{1,5},{5... | collective-permute-start | bytes 3145736 | tf_op jit(solution)/shard_map/ppermute | solution.py:10
  35.0 24.4 %collective-permute-start.1 = (f32[256,1024]{1,0:T(8,128)S(1)}, f32[256,1024]{1,0:T(8,128)S(1)}, u32[]{:S(2)}, u32[]{:S(2)}) collective-permute-start(f32[256,1024]{1,0:T(8,128)S(1)} %fusion.44), channel_id=1, source_target_pairs={{0,8},{4,12},{8,0},{12,4},{16,24},{20,28},{24,16},{28,20},{1,9},{5... | collective-permute-start | bytes 3145736 | tf_op jit(solution)/shard_map/ppermute | solution.py:10
  60.6 261.9 %all-reduce.3.cloned.1.call-start = ((), (), s32[]{:S(2)}) async-start(), calls=%async_computation.3 | async-start | bytes 24117248 | tf_op jit(solution)/shard_map/psum | solution.py:127
  110.2 237.4 %all-gather.8.cloned.1.call-start = ((), (), s32[]{:S(2)}) async-start(), calls=%async_computation.2 | async-start | bytes 2621440 | tf_op jit(solution)/shard_map/all_gather | solution.py:105
  144.0 73.7 %collective-permute-start.2 = (f32[256,2048]{0,1:T(8,128)}, f32[256,2048]{0,1:T(8,128)}, u32[]{:S(2)}, u32[]{:S(2)}) collective-permute-start(f32[256,2048]{0,1:T(8,128)} %fusion.6), channel_id=1, source_target_pairs={{0,4},{4,0},{8,12},{12,8},{16,20},{20,16},{24,28},{28,24},{1,5},{5... | collective-permute-start | bytes 6291464 | tf_op jit(solution)/shard_map/ppermute | solution.py:10
  148.1 55.0 %collective-permute-start.4 = (f32[512,256]{1,0:T(8,128)S(1)}, f32[512,256]{1,0:T(8,128)S(1)}, u32[]{:S(2)}, u32[]{:S(2)}) collective-permute-start(f32[512,256]{1,0:T(8,128)S(1)} %fusion.14), channel_id=1, source_target_pairs={{0,4},{4,0},{8,12},{12,8},{16,20},{20,16},{24,28},{28,24},{1,5},{5... | collective-permute-start | bytes 1572872 | tf_op jit(solution)/shard_map/ppermute | solution.py:10
  203.4 13.3 %collective-permute-start.5 = (f32[512,256]{1,0:T(8,128)S(1)}, f32[512,256]{1,0:T(8,128)S(1)}, u32[]{:S(2)}, u32[]{:S(2)}) collective-permute-start(f32[512,256]{1,0:T(8,128)S(1)} %fusion.43), channel_id=1, source_target_pairs={{0,8},{4,12},{8,0},{12,4},{16,24},{20,28},{24,16},{28,20},{1,9},{5... | collective-permute-start | bytes 1572872 | tf_op jit(solution)/shard_map/ppermute | solution.py:10
  217.6 340.9 %all-gather.6.cloned.1.call-start = ((), (), s32[]{:S(2)}) async-start(), calls=%async_computation.1 | async-start | bytes 10485760 | tf_op jit(solution)/shard_map/all_gather | solution.py:104
  220.3 46.2 %collective-permute-start.3 = (f32[256,2048]{0,1:T(8,128)S(1)}, f32[256,2048]{0,1:T(8,128)S(1)}, u32[]{:S(2)}, u32[]{:S(2)}) collective-permute-start(f32[256,2048]{0,1:T(8,128)S(1)} %fusion.42), channel_id=1, source_target_pairs={{0,8},{4,12},{8,0},{12,4},{16,24},{20,28},{24,16},{28,20},{1,9},{5... | collective-permute-start | bytes 6291464 | tf_op jit(solution)/shard_map/ppermute | solution.py:10
  322.5 300.8 %collective-permute-start.6 = (f32[1024,2048]{0,1:T(8,128)}, f32[1024,2048]{0,1:T(8,128)}, u32[]{:S(2)}, u32[]{:S(2)}) collective-permute-start(f32[1024,2048]{0,1:T(8,128)} %get-tuple-element.25), channel_id=1, source_target_pairs={{0,4},{4,0},{8,12},{12,8},{16,20},{20,16},{24,28},{28,24},{1,5},{5... | collective-permute-start | bytes 25165832 | tf_op jit(solution)/shard_map/ppermute | solution.py:10
  324.0 225.5 %collective-permute-start.7 = (f32[2048,256]{1,0:T(8,128)}, f32[2048,256]{1,0:T(8,128)}, u32[]{:S(2)}, u32[]{:S(2)}) collective-permute-start(f32[2048,256]{1,0:T(8,128)} %get-tuple-element.26), channel_id=1, source_target_pairs={{0,4},{4,0},{8,12},{12,8},{16,20},{20,16},{24,28},{28,24},{1,5},{5... | collective-permute-start | bytes 6291464 | tf_op jit(solution)/shard_map/ppermute | solution.py:10
  324.5 225.0 %copy-start.16 = (f32[2048,256]{1,0:T(8,128)S(1)}, f32[2048,256]{1,0:T(8,128)}, u32[]{:S(2)}) copy-start(f32[2048,256]{1,0:T(8,128)} %get-tuple-element.26) | copy-start | bytes 6291460
  558.5 25.9 %copy-start.5 = (f32[128,8,4,256]{3,1,2,0:T(8,128)S(1)}, f32[128,8,4,256]{3,1,2,0:T(8,128)}, u32[]{:S(2)}) copy-start(f32[128,8,4,256]{3,1,2,0:T(8,128)} %copy.55) | copy-start | bytes 12582916
  558.5 25.9 %copy-start.13 = (f32[1024,2048]{0,1:T(8,128)S(1)}, f32[1024,2048]{0,1:T(8,128)}, u32[]{:S(2)}) copy-start(f32[1024,2048]{0,1:T(8,128)} %all-gather.6.cloned.1.call-done) | copy-start | bytes 25165828
  622.2 18.5 %slice-start = ((s8[8388608]{0:T(1024)(128)(4,1)}), s8[4194304]{0:T(1024)(128)(4,1)S(1)}, s32[]{:S(2)}) async-start(s8[8388608]{0:T(1024)(128)(4,1)} %bitcast.80), calls=%async_computation.4 | async-start | bytes 8388608
  623.3 17.4 %slice-start.1 = ((s8[8388608]{0:T(1024)(128)(4,1)}), s8[4194304]{0:T(1024)(128)(4,1)S(1)}, s32[]{:S(2)}) async-start(s8[8388608]{0:T(1024)(128)(4,1)} %bitcast.80), calls=%async_computation.5 | async-start | bytes 8388608
  623.3 33.8 %slice-start.2 = ((s8[6291456]{0:T(1024)(128)(4,1)}), s8[4194304]{0:T(1024)(128)(4,1)S(1)}, s32[]{:S(2)}) async-start(s8[6291456]{0:T(1024)(128)(4,1)} %bitcast.82), calls=%async_computation.6 | async-start | bytes 8388608
  640.7 16.3 %slice-start.3 = ((s8[6291456]{0:T(1024)(128)(4,1)}), s8[2097152]{0:T(1024)(128)(4,1)S(1)}, s32[]{:S(2)}) async-start(s8[6291456]{0:T(1024)(128)(4,1)} %bitcast.82), calls=%async_computation.7 | async-start | bytes 4194304
  686.0 17.6 %copy-start.14 = (f32[1536,256]{1,0:T(8,128)S(1)}, f32[1536,256]{1,0:T(8,128)}, u32[]{:S(2)}) copy-start(f32[1536,256]{1,0:T(8,128)} %param.16) | copy-start | bytes 4718596
  686.0 18.9 %copy-start.1 = (s32[4,4]{1,0:T(4,128)S(1)}, s32[4,4]{1,0:T(4,128)}, u32[]{:S(2)}) copy-start(s32[4,4]{1,0:T(4,128)} %param.14) | copy-start | bytes 196
  (10 other events, 74.3 us)
Sparse Core Ops, SparseCore 0:
  60.7 35.6 all-gather.3
  110.3 212.1 all-reduce.2
  324.6 22.8 all-gather.7
  348.9 58.2 all-gather.5
where the time goes:
time: 720 us; the launch traced here: 712 us
  waiting for transfers between devices  430 us (60%)
  matrix products  143 us (20%)
  local copies, waits for them, and re-layouts  86.5 us (12%)
  other arithmetic  24.8 us (3%)
  between operations  14.7 us (2%)
  starting transfers between devices  12.9 us (2%)
    ppermute x8, waiting for transfers between devices, from_partner(): lax.ppermute(value, axis, [(i, i ^ 1 << bit) for i in range(lax.axis_size...  355 us
    psum x1, waiting for transfers between devices, local(): summed_terms = lax.psum(partial_value, 'rows')  54.4 us
    dot_general x2, matrix products, child_cov(): jnp.dot(parent_cov, chosen, precision=HIGH, preferred_element_type=jnp.fl...  43.3 us
    gather x4, local copies, waits for them, and re-layouts, select_blocks(): jnp.take(panel_cols.reshape(rows_total, local_count, block_size), wanted,...  30.7 us
    dot_general x2, matrix products, child_cov(): jnp.dot(chosen.T, product, precision=HIGH, preferred_element_type=jnp.flo...  30.3 us
    unnamed x55, local copies, waits for them, and re-layouts  28.7 us
    dot_general x3, matrix products, marg_terms(): jnp.einsum('sai,saj->aij', panel_cols.reshape(rows_total, block_count, bl...  27.1 us
    dot_general x1, matrix products, local(): jnp.dot(low_cov, panel_low, precision=HIGH, preferred_element_type=jnp.fl...  22.3 us
  transfers between devices with their start and end apart: 12, of which 9 were waited for; matrix products, arithmetic and copies ran while one was open for 22% of the time, Pallas kernels for 0%

commit v1 on v0

--- a/solution.py
+++ b/solution.py
@@ -124,7 +124,11 @@
     partial_value = marg_terms(panel_rows, cross_top, block_size)
     piece_rows = partial_value.shape[0] // row_count
     own_diag = lax.dynamic_slice_in_dim(diag_top, rows_index * piece_rows, piece_rows, 0)
-    summed_terms = lax.psum(partial_value, "rows")
+    summed_terms = partial_value
+    for hop in (1, 2):
+        summed_terms = summed_terms + lax.ppermute(
+            summed_terms, "rows", [(dev, dev ^ hop) for dev in range(4)]
+        )
     marginal_top = own_diag - lax.dynamic_slice_in_dim(
         summed_terms, rows_index * piece_rows, piece_rows, 0
     )

time: 720 us -> 621 us (0.86)
  waiting for transfers between devices: 430 us -> 352 us
  matrix products: 143 us -> 126 us
    psum x1, waiting for transfers between devices: 54.4 us -> 0.02 us  [local(): summed = lax.psum((chosen_mid, chosen_mid_diag), 'rows')]
    ppermute x8, waiting for transfers between devices: 355 us -> 329 us  [from_partner(): lax.ppermute(value, axis, [(i, i ^ 1 << bit) for i in range(lax.axis_size...]
    all_gather x1, waiting for transfers between devices: 3.92 us -> 16 us  [local(): lax.all_gather(pieces[0], 'rows', axis=0, tiled=True)]
    all_gather x1, waiting for transfers between devices: 16.3 us -> 4.72 us  [local(): lax.all_gather(pieces[2], 'rows', axis=0, tiled=True)]
    dot_general x3, matrix products: 27.1 us -> 17 us  [marg_terms(): jnp.einsum('sai,saj->aij', panel_cols.reshape(rows_total, block_count, bl...]
    dot_general x2, matrix products: 43.3 us -> 34 us  [child_cov(): jnp.dot(parent_cov, chosen, precision=HIGH, preferred_element_type=jnp.fl...]
    unnamed x55 -> x43, local copies, waits for them, and re-layouts: 28.7 us -> 28.2 us
  transfers between devices with their start and end apart: 12 -> 14, of which waited for: 9 -> 9; matrix products, arithmetic and copies ran while one was open for 22% -> 20% of each run, Pallas kernels for 0% -> 0%
where the time goes in v1:
time: 621 us; the launch traced here: 615 us
  waiting for transfers between devices  352 us (57%)
  matrix products  126 us (20%)
  local copies, waits for them, and re-layouts  84.4 us (14%)
  other arithmetic  25.3 us (4%)
  between operations  14.4 us (2%)
  starting transfers between devices  12.6 us (2%)
    ppermute x8, waiting for transfers between devices, from_partner(): lax.ppermute(value, axis, [(i, i ^ 1 << bit) for i in range(lax.axis_size...  329 us
    dot_general x2, matrix products, child_cov(): jnp.dot(parent_cov, chosen, precision=HIGH, preferred_element_type=jnp.fl...  34 us
    dot_general x2, matrix products, child_cov(): jnp.dot(chosen.T, product, precision=HIGH, preferred_element_type=jnp.flo...  32.4 us
    gather x4, local copies, waits for them, and re-layouts, select_blocks(): jnp.take(panel_cols.reshape(rows_total, local_count, block_size), wanted,...  30 us
    unnamed x43, local copies, waits for them, and re-layouts  28.2 us
    dot_general x1, matrix products, local(): jnp.dot(low_cov, panel_low, precision=HIGH, preferred_element_type=jnp.fl...  22.5 us
    dot_general x3, matrix products, marg_terms(): jnp.einsum('sai,saj->aij', panel_cols.reshape(rows_total, block_count, bl...  17 us
    all_gather x1, waiting for transfers between devices, local(): lax.all_gather(pieces[0], 'rows', axis=0, tiled=True)  16 us
  transfers between devices with their start and end apart: 14, of which 9 were waited for; matrix products, arithmetic and copies ran while one was open for 20% of the time, Pallas kernels for 0%

profile of v1, /device:TPU:0, one launch (start us, length us, event | category | flops | bytes accessed | tf_op | source)
XLA Modules:
  0.0 614.8 jit_solution(3641425093928977869)
XLA Ops:
  19.0 9.2 %copy.46 = f32[1024,8,256]{0,2,1:T(8,128)} copy(f32[1024,8,256]{2,0,1:T(8,128)} %bitcast.67) | data formatting | bytes 16777216 | tf_op jit(solution)/shard_map/jit(_take)/gather | solution.py:25
  29.3 5.9 fusion
  41.5 23.2 %collective-permute-done = f32[256,1024]{1,0:T(8,128)S(1)} collective-permute-done((f32[256,1024]{1,0:T(8,128)S(1)}, f32[256,1024]{1,0:T(8,128)S(1)}, u32[]{:S(2)}, u32[]{:S(2)}) %collective-permute-start) | collective-permute-done | bytes 1048608 | tf_op jit(solution)/shard_map/ppermute | solution.py:10
  66.7 22.6 %collective-permute-done.1 = f32[256,1024]{1,0:T(8,128)S(1)} collective-permute-done((f32[256,1024]{1,0:T(8,128)S(1)}, f32[256,1024]{1,0:T(8,128)S(1)}, u32[]{:S(2)}, u32[]{:S(2)}) %collective-permute-start.1) | collective-permute-done | bytes 1048608 | tf_op jit(solution)/shard_map/ppermute | solution.py:10
  91.3 6.6 %copy.39 = f32[1024,1536]{0,1:T(8,128)} copy(f32[1024,1536]{1,0:T(8,128)} %param.10) | data formatting | bytes 12582912 | tf_op args[1]
  97.9 6.7 %copy.40 = f32[1024,6,256]{2,0,1:T(8,128)} copy(f32[1024,6,256]{0,2,1:T(8,128)} %bitcast.73) | data formatting | bytes 12582912 | tf_op jit(solution)/shard_map/reshape | solution.py:25
  104.6 7.2 %gather_fusion.1 = f32[8,1024,256]{2,1,0:T(8,128)} fusion(f32[1024,6,256]{2,0,1:T(8,128)} %copy.40, s32[1024]{0:T(1024)S(1)} %pad_clamp_fusion.2), kind=kCustom, calls=%fused_computation.1 | custom fusion | bytes 16777248 | tf_op jit(solution)/shard_map/jit(_take)/gather | solution.py:25
  111.8 9.2 %copy.41 = f32[1024,8,256]{0,2,1:T(8,128)} copy(f32[1024,8,256]{2,0,1:T(8,128)} %bitcast.68) | data formatting | bytes 16777216 | tf_op jit(solution)/shard_map/jit(_take)/gather | solution.py:25
  128.9 53.2 %collective-permute-done.6 = f32[512,256]{1,0:T(8,128)S(1)} collective-permute-done((f32[512,256]{1,0:T(8,128)S(1)}, f32[512,256]{1,0:T(8,128)S(1)}, u32[]{:S(2)}, u32[]{:S(2)}) %collective-permute-start.6) | collective-permute-done | bytes 524320 | tf_op jit(solution)/shard_map/ppermute | solution.py:10
  183.5 10.7 %collective-permute-done.7 = f32[512,256]{1,0:T(8,128)S(1)} collective-permute-done((f32[512,256]{1,0:T(8,128)S(1)}, f32[512,256]{1,0:T(8,128)S(1)}, u32[]{:S(2)}, u32[]{:S(2)}) %collective-permute-start.7) | collective-permute-done | bytes 524320 | tf_op jit(solution)/shard_map/ppermute | solution.py:10
  199.3 43.9 %collective-permute-done.5 = f32[256,2048]{0,1:T(8,128)S(1)} collective-permute-done((f32[256,2048]{0,1:T(8,128)S(1)}, f32[256,2048]{0,1:T(8,128)S(1)}, u32[]{:S(2)}, u32[]{:S(2)}) %collective-permute-start.5) | collective-permute-done | bytes 2097184 | tf_op jit(solution)/shard_map/ppermute | solution.py:10
  247.4 16.0 %all-gather.4.cloned.1.call-done = f32[1024,1024]{1,0:T(8,128)} async-done(((f32[256,1024]{1,0:T(8,128)}), f32[1024,1024]{1,0:T(8,128)}) %all-gather.4.cloned.1.call-update) | async-done | bytes 4194320 | tf_op jit(solution)/shard_map/all_gather | solution.py:103
  263.5 7.9 %convolution_negate_fusion.1 = f32[256,1536]{1,0:T(8,128)S(1)} fusion(f32[1024,1536]{1,0:T(8,128)} %param.10, f32[1024,1024]{1,0:T(8,128)} %all-gather.4.cloned.1.call-done, s32[]{:T(128)S(6)} %select_n.181), kind=kOutput, calls=%fused_computation.15 | convolution fusion | flops 4832231424 | bytes 8912900 | tf_op jit(solution)/shard_map/dot_general | solution.py:122
  280.5 6.6 %copy.48 = f32[1024,1536]{0,1:T(8,128)} copy(f32[1024,1536]{1,0:T(8,128)} %param.15) | data formatting | bytes 12582912 | tf_op args[6]
  293.1 175.8 %collective-permute-done.9 = f32[2048,256]{1,0:T(8,128)} collective-permute-done((f32[2048,256]{1,0:T(8,128)}, f32[2048,256]{1,0:T(8,128)}, u32[]{:S(2)}, u32[]{:S(2)}) %collective-permute-start.9) | collective-permute-done | bytes 2097184 | tf_op jit(solution)/shard_map/ppermute | solution.py:10
  480.2 17.3 %fusion.4 = f32[1024,1024]{1,0:T(8,128)S(1)} fusion(f32[1024,1024]{1,0:T(8,128)} %all-gather.4.cloned.1.call-done, f32[1024,2048]{0,1:T(8,128)} %all-gather.6.cloned.1.call-done, s32[]{:T(128)S(6)} %select_n.193), kind=kOutput, calls=%fused_computation.13 | convolution fusion | flops 12884901888 | bytes 12582916 | tf_op jit(solution)/shard_map/dot_general | solution.py:37
  497.5 16.1 %fusion.8 = f32[1024,1024]{1,0:T(8,128)S(1)} fusion(f32[1024,1024]{1,0:T(8,128)S(1)} %bitcast.76, f32[1024,1024]{1,0:T(8,128)S(1)} %fusion.4, f32[1024,2048]{0,1:T(8,128)} %all-gather.6.cloned.1.call-done, s32[]{:T(128)S(6)} %select_n.193), kind=kOutput, calls=%fused_computation.22 | convolution fusion | flops 12885950464 | bytes 16777220 | tf_op jit(solution)/shard_map/dot_general | solution.py:38
  513.7 12.2 %convolution_negate_fusion.2 = f32[1024,768]{0,1:T(8,128)} fusion(f32[1024,1024]{1,0:T(8,128)S(1)} %fusion.8, f32[1024,768]{1,0:T(8,128)S(1)} %copy-done.9), kind=kOutput, calls=%fused_computation.23 | convolution fusion | flops 9664462848 | bytes 10485760 | tf_op jit(solution)/shard_map/dot_general | solution.py:141
  525.9 16.7 %fusion.11 = f32[1024,1024]{1,0:T(8,128)S(1)} fusion(f32[1024,1024]{1,0:T(8,128)S(1)} %fusion.8, f32[1024,2048]{0,1:T(8,128)} %collective-permute-done.8, s32[]{:T(128)S(6)} %select_n.204, f32[1024,2048]{0,1:T(8,128)S(1)} %bitcast.82), kind=kOutput, calls=%fused_computation.25 | convolution fusion | flops 12885950464 | bytes 16777220 | tf_op jit(solution)/shard_map/dot_general | solution.py:37
  542.6 16.3 %fusion.12 = f32[1024,1024]{1,0:T(8,128)S(1)} fusion(f32[1024,1024]{1,0:T(8,128)S(1)} %fusion.11, f32[1024,2048]{0,1:T(8,128)} %collective-permute-done.8, s32[]{:T(128)S(6)} %select_n.204, f32[1024,2048]{0,1:T(8,128)S(1)} %bitcast.82), kind=kOutput, calls=%fused_computation.26 | convolution fusion | flops 12885950464 | bytes 16777220 | tf_op jit(solution)/shard_map/dot_general | solution.py:38
  558.9 22.5 %convolution_negate_fusion = f32[1024,1536]{1,0:T(8,128)} fusion(f32[1024,1536]{1,0:T(8,128)S(1)} %bitcast.84, f32[1024,1024]{1,0:T(8,128)S(1)} %fusion.12, f32[1024,1024]{1,0:T(8,128)S(1)} %bitcast.90), kind=kOutput, calls=%fused_computation.8 | convolution fusion | flops 19329974272 | bytes 20971520 | tf_op jit(solution)/shard_map/dot_general | solution.py:147
  581.5 6.6 %copy.47 = f32[1024,1536]{0,1:T(8,128)} copy(f32[1024,1536]{1,0:T(8,128)} %convolution_negate_fusion) | data formatting | bytes 12582912 | tf_op jit(solution)/shard_map/neg | solution.py:147
  591.9 5.3 fusion.27
  598.2 8.4 %fusion.28 = f32[6,256,256]{1,2,0:T(8,128)S(1)} fusion(f32[1024,6,256]{0,2,1:T(8,128)S(1)} %bitcast.72, f32[1024,6,256]{0,2,1:T(8,128)} %bitcast.71), kind=kOutput, calls=%fused_computation.80 | convolution fusion | flops 4831838208 | bytes 14155776 | tf_op jit(solution)/shard_map/sai,saj->aij/dot_general | solution.py:45
  (125 shorter events, 74.1 us)
Async XLA Ops:
  7.2 83.4 %copy-start = (s32[4,4]{1,0:T(4,128)S(1)}, s32[4,4]{1,0:T(4,128)}, u32[]{:S(2)}) copy-start(s32[4,4]{1,0:T(4,128)} %param.14) | copy-start | bytes 196
  7.2 237.7 %all-reduce.3.cloned.1.call-start = ((), (), s32[]{:S(2)}) async-start(), calls=%async_computation.3 | async-start | bytes 20971520 | tf_op jit(solution)/shard_map/psum | solution.py:116
  19.0 9.6 %copy-start.5 = (f32[768,256]{1,0:T(8,128)S(1)}, f32[768,256]{1,0:T(8,128)}, u32[]{:S(2)}) copy-start(f32[768,256]{1,0:T(8,128)} %param.13) | copy-start | bytes 2359300
  37.1 226.4 %all-gather.4.cloned.1.call-start = ((), (), s32[]{:S(2)}) async-start(), calls=%async_computation | async-start | bytes 5242880 | tf_op jit(solution)/shard_map/all_gather | solution.py:103
  38.5 26.2 %collective-permute-start = (f32[256,1024]{1,0:T(8,128)S(1)}, f32[256,1024]{1,0:T(8,128)S(1)}, u32[]{:S(2)}, u32[]{:S(2)}) collective-permute-start(f32[256,1024]{1,0:T(8,128)S(1)} %constant_dynamic-slice_fusion.2), channel_id=1, source_target_pairs={{0,4},{4,0},{8,12},{12,8},{16,20},{20,16},{24,28},{28,24},{1,5},{5... | collective-permute-start | bytes 3145736 | tf_op jit(solution)/shard_map/ppermute | solution.py:10
  64.9 24.5 %collective-permute-start.1 = (f32[256,1024]{1,0:T(8,128)S(1)}, f32[256,1024]{1,0:T(8,128)S(1)}, u32[]{:S(2)}, u32[]{:S(2)}) collective-permute-start(f32[256,1024]{1,0:T(8,128)S(1)} %fusion.45), channel_id=1, source_target_pairs={{0,8},{4,12},{8,0},{12,4},{16,24},{20,28},{24,16},{28,20},{1,9},{5... | collective-permute-start | bytes 3145736 | tf_op jit(solution)/shard_map/ppermute | solution.py:10
  90.5 201.3 %all-gather.8.cloned.1.call-start = ((), (), s32[]{:S(2)}) async-start(), calls=%async_computation.2 | async-start | bytes 2621440 | tf_op jit(solution)/shard_map/all_gather | solution.py:105
  124.3 71.4 %collective-permute-start.4 = (f32[256,2048]{0,1:T(8,128)}, f32[256,2048]{0,1:T(8,128)}, u32[]{:S(2)}, u32[]{:S(2)}) collective-permute-start(f32[256,2048]{0,1:T(8,128)} %fusion.6), channel_id=1, source_target_pairs={{0,4},{4,0},{8,12},{12,8},{16,20},{20,16},{24,28},{28,24},{1,5},{5... | collective-permute-start | bytes 6291464 | tf_op jit(solution)/shard_map/ppermute | solution.py:10
  128.2 53.9 %collective-permute-start.6 = (f32[512,256]{1,0:T(8,128)S(1)}, f32[512,256]{1,0:T(8,128)S(1)}, u32[]{:S(2)}, u32[]{:S(2)}) collective-permute-start(f32[512,256]{1,0:T(8,128)S(1)} %fusion.14), channel_id=1, source_target_pairs={{0,4},{4,0},{8,12},{12,8},{16,20},{20,16},{24,28},{28,24},{1,5},{5... | collective-permute-start | bytes 1572872 | tf_op jit(solution)/shard_map/ppermute | solution.py:10
  182.3 12.0 %collective-permute-start.7 = (f32[512,256]{1,0:T(8,128)S(1)}, f32[512,256]{1,0:T(8,128)S(1)}, u32[]{:S(2)}, u32[]{:S(2)}) collective-permute-start(f32[512,256]{1,0:T(8,128)S(1)} %fusion.44), channel_id=1, source_target_pairs={{0,8},{4,12},{8,0},{12,4},{16,24},{20,28},{24,16},{28,20},{1,9},{5... | collective-permute-start | bytes 1572872 | tf_op jit(solution)/shard_map/ppermute | solution.py:10
  195.1 285.1 %all-gather.6.cloned.1.call-start = ((), (), s32[]{:S(2)}) async-start(), calls=%async_computation.1 | async-start | bytes 10485760 | tf_op jit(solution)/shard_map/all_gather | solution.py:104
  198.4 44.8 %collective-permute-start.5 = (f32[256,2048]{0,1:T(8,128)S(1)}, f32[256,2048]{0,1:T(8,128)S(1)}, u32[]{:S(2)}, u32[]{:S(2)}) collective-permute-start(f32[256,2048]{0,1:T(8,128)S(1)} %fusion.43), channel_id=1, source_target_pairs={{0,8},{4,12},{8,0},{12,4},{16,24},{20,28},{24,16},{28,20},{1,9},{5... | collective-permute-start | bytes 6291464 | tf_op jit(solution)/shard_map/ppermute | solution.py:10
  244.9 281.0 %collective-permute-start.8 = (f32[1024,2048]{0,1:T(8,128)}, f32[1024,2048]{0,1:T(8,128)}, u32[]{:S(2)}, u32[]{:S(2)}) collective-permute-start(f32[1024,2048]{0,1:T(8,128)} %get-tuple-element.24), channel_id=1, source_target_pairs={{0,4},{4,0},{8,12},{12,8},{16,20},{20,16},{24,28},{28,24},{1,5},{5... | collective-permute-start | bytes 25165832 | tf_op jit(solution)/shard_map/ppermute | solution.py:10
  276.3 3.7 collective-permute-start.2
  276.7 192.2 %collective-permute-start.9 = (f32[2048,256]{1,0:T(8,128)}, f32[2048,256]{1,0:T(8,128)}, u32[]{:S(2)}, u32[]{:S(2)}) collective-permute-start(f32[2048,256]{1,0:T(8,128)} %get-tuple-element.25), channel_id=1, source_target_pairs={{0,4},{4,0},{8,12},{12,8},{16,20},{20,16},{24,28},{28,24},{1,5},{5... | collective-permute-start | bytes 6291464 | tf_op jit(solution)/shard_map/ppermute | solution.py:10
  280.2 198.0 %collective-permute-start.3 = (f32[1536,256]{1,0:T(8,128)S(1)}, f32[1536,256]{1,0:T(8,128)}, u32[]{:S(2)}, u32[]{:S(2)}) collective-permute-start(f32[1536,256]{1,0:T(8,128)S(1)} %bitcast_add_fusion), channel_id=1, source_target_pairs={{0,2},{1,3},{2,0},{3,1},{4,6},{5,7},{6,4},{7,5},{8,10},{9,11},{10,... | collective-permute-start | bytes 4718600 | tf_op jit(solution)/shard_map/ppermute | solution.py:129
  480.2 17.3 %copy-start.4 = (f32[128,8,4,256]{3,1,2,0:T(8,128)S(1)}, f32[128,8,4,256]{3,1,2,0:T(8,128)}, u32[]{:S(2)}) copy-start(f32[128,8,4,256]{3,1,2,0:T(8,128)} %copy.55) | copy-start | bytes 12582916
  480.2 45.7 %slice-start = ((s8[8388608]{0:T(1024)(128)(4,1)}), s8[4194304]{0:T(1024)(128)(4,1)S(1)}, s32[]{:S(2)}) async-start(s8[8388608]{0:T(1024)(128)(4,1)} %bitcast.81), calls=%async_computation.4 | async-start | bytes 8388608
  497.5 16.2 %copy-start.9 = (f32[1024,768]{1,0:T(8,128)S(1)}, f32[1024,768]{1,0:T(8,128)}, u32[]{:S(2)}) copy-start(f32[1024,768]{1,0:T(8,128)} %param.12) | copy-start | bytes 9437188
  497.5 28.3 %slice-start.1 = ((s8[8388608]{0:T(1024)(128)(4,1)}), s8[4194304]{0:T(1024)(128)(4,1)S(1)}, s32[]{:S(2)}) async-start(s8[8388608]{0:T(1024)(128)(4,1)} %bitcast.81), calls=%async_computation.5 | async-start | bytes 8388608
  525.9 33.0 %slice-start.2 = ((s8[6291456]{0:T(1024)(128)(4,1)}), s8[4194304]{0:T(1024)(128)(4,1)S(1)}, s32[]{:S(2)}) async-start(s8[6291456]{0:T(1024)(128)(4,1)} %bitcast.83), calls=%async_computation.6 | async-start | bytes 8388608
  542.6 16.3 %slice-start.3 = ((s8[6291456]{0:T(1024)(128)(4,1)}), s8[2097152]{0:T(1024)(128)(4,1)S(1)}, s32[]{:S(2)}) async-start(s8[6291456]{0:T(1024)(128)(4,1)} %bitcast.83), calls=%async_computation.7 | async-start | bytes 4194304
  542.6 16.3 %copy-start.8 = (f32[128,8,4,256]{3,1,2,0:T(8,128)S(1)}, f32[128,8,4,256]{3,1,2,0:T(8,128)}, u32[]{:S(2)}) copy-start(f32[128,8,4,256]{3,1,2,0:T(8,128)} %copy.57) | copy-start | bytes 12582916
  598.2 9.8 %copy-start.1 = (s32[4,4]{1,0:T(4,128)S(1)}, s32[4,4]{1,0:T(4,128)}, u32[]{:S(2)}) copy-start(s32[4,4]{1,0:T(4,128)} %param.14) | copy-start | bytes 196
  (6 other events, 34.0 us)
Sparse Core Ops, SparseCore 0:
  37.2 189.4 all-reduce.2
  228.8 34.6 all-gather.3
  265.6 26.1 all-gather.7
  293.2 73.8 all-gather.5
